TPU v7x, 32 devices: a whole 2x2x4 slice. The times are simulated.
32 devices in a mesh: sph: 8 (over z, core), fit: 4 (over y, x).
Axes of the slice: x: 2, y: 2, z: 4, core: 2. Of those that a mesh axis runs over, the one named last changes fastest.
Arguments:
- tiles: bfloat16 [1024, 163840], P('fit', 'sph'), may hold values from -0.1875 to 0.1875
- coefs: bfloat16 [16, 1024], P(None, 'fit'), may hold values from -6 to 6
- centres: float32 [3, 512], P(None, ('sph', 'fit'))
- radii: float32 [512], P(('sph', 'fit')), may hold values from 1 to 1.6
- neighbours: int32 [512, 16], P(('sph', 'fit')), may hold values from 0 to 511, as said below
- counts: int32 [512], P(('sph', 'fit')), may hold values from 1 to 16
Outputs:
- moments: float32 [512, 16, 49], P(('sph', 'fit'))
- fock: float32 [16, 1024], P(None, 'fit')
Inputs may be any that keep to these rules, and one draw needn't show every extreme that they name: `neighbours`: every entry j of row i satisfies |j - i| <= 8; the first counts[i] entries of a row are distinct and differ from i, the rest equal i.
All inputs are finite; a program needn't handle non-finite values.
Results may differ from a plain program's by a relative error of at most 0.00086.
Values may be sent and summed in bfloat16 or wider, within the bound.
No kernel may reach another device: no remote copies, remote signals or barrier semaphores. Data moves between devices by JAX's collectives and lax.ppermute only.
A program may use at most 192 MiB of HBM per device.

v0:
```python
import math
import jax
import jax.numpy as jnp
from jax import lax
from jax.sharding import PartitionSpec as P

DEGREE = 6
NTH = 16
NPHI = 20
NG = 320
NDENS = 16
band = 0.1


def with_halo(array, sides, width):
    for axis, dim in sides:
        count, length = (lax.axis_size(axis), array.shape[dim])
        up = [(i, (i + 1) % count) for i in range(count - 1)]
        down = [(j, i) for i, j in up]
        last = lax.slice_in_dim(array, length - width, length, axis=dim)
        initial = lax.slice_in_dim(array, 0, width, axis=dim)
        before = lax.ppermute(last, axis, up)
        after = lax.ppermute(initial, axis, down)
        array = jnp.concatenate([before, array, after], axis=dim)
    return array


def solid(coord_x, coord_y, coord_z):
    radius_squared = coord_x * coord_x + coord_y * coord_y + coord_z * coord_z
    cos_part = [jnp.ones_like(coord_x)]
    sin_part = [jnp.zeros_like(coord_x)]
    for harmonic_order in range(1, DEGREE + 1):
        cprev = cos_part[-1]
        sprev = sin_part[-1]
        cos_part.append(cprev * coord_x - sprev * coord_y)
        sin_part.append(cprev * coord_y + sprev * coord_x)
    result = [None] * (DEGREE + 1) ** 2
    for harmonic_order in range(DEGREE + 1):
        dfact = 1.0
        for odd in range(1, 2 * harmonic_order, 2):
            dfact = dfact * odd
        lower_term = None
        current = dfact * jnp.ones_like(coord_x)
        for harmonic_degree in range(harmonic_order, DEGREE + 1):
            if harmonic_degree > harmonic_order:
                next_term = (2 * harmonic_degree - 1) * coord_z * current
                if lower_term is not None:
                    next_term = (
                        next_term
                        - (harmonic_degree + harmonic_order - 1) * radius_squared * lower_term
                    )
                lower_term = current
                current = next_term / (harmonic_degree - harmonic_order)
            scale = math.sqrt(
                (2 * harmonic_degree + 1)
                / (4 * math.pi)
                * math.factorial(harmonic_degree - harmonic_order)
                / math.factorial(harmonic_degree + harmonic_order)
            )
            if harmonic_order == 0:
                result[harmonic_degree * harmonic_degree + harmonic_degree] = scale * current
            else:
                result[harmonic_degree * harmonic_degree + harmonic_degree + harmonic_order] = (
                    math.sqrt(2.0) * scale * current * cos_part[harmonic_order]
                )
                result[harmonic_degree * harmonic_degree + harmonic_degree - harmonic_order] = (
                    math.sqrt(2.0) * scale * current * sin_part[harmonic_order]
                )
    return result


def grid_tables():
    polar_index = jnp.arange(NTH, dtype=jnp.float32)
    polar_nodes = -1.0 + (2.0 * polar_index + 1.0) / NTH
    angles = (jnp.arange(NPHI, dtype=jnp.float32) + 0.5) * (2.0 * math.pi / NPHI)
    cosines = jnp.repeat(polar_nodes, NPHI)
    sines = jnp.sqrt(1.0 - cosines * cosines)
    azimuth = jnp.tile(angles, NTH)
    dirs = jnp.stack([sines * jnp.cos(azimuth), sines * jnp.sin(azimuth), cosines])
    weights = jnp.full((NTH * NPHI,), 4.0 * math.pi / (NTH * NPHI), dtype=jnp.float32)
    ysurf = jnp.stack(solid(dirs[0], dirs[1], dirs[2]))
    levels = jnp.asarray(
        [
            float(harmonic_degree)
            for harmonic_degree in range(DEGREE + 1)
            for harmonic_order in range(2 * harmonic_degree + 1)
        ],
        dtype=jnp.float32,
    )
    couple = 4.0 * math.pi / (2.0 * levels + 1.0)
    invert = (2.0 * levels + 1.0) / (4.0 * math.pi)
    return (dirs, weights, ysurf, couple, invert)


def block_basis(own, near, valid, dirs, couple):
    centre = own[:3]
    radius = own[3]
    offset = centre[:, :, None] - near[:3]
    near_rad = jnp.where(valid > 0, near[3], 1.0)
    vec = (offset[:, :, :, None] + radius[None, :, None, None] * dirs[:, None, None, :]) / near_rad[
        None, :, :, None
    ]
    dist = jnp.sqrt(jnp.sum(vec * vec, axis=0))
    ramp = jnp.clip((1.0 - dist) / band, 0.0, 1.0)
    switch = ramp * ramp * (3.0 - 2.0 * ramp) * valid[:, :, None]
    harm = jnp.stack(solid(vec[0], vec[1], vec[2]), axis=2)
    basis = harm * couple[None, None, :, None] * switch[:, :, None, :]
    uncovered = jnp.maximum(0.0, 1.0 - jnp.sum(switch, axis=1))
    return (basis, uncovered)


def block_rhs(weighted, uncovered, potential):
    return -jnp.einsum(
        "lp,sdp->sdl", weighted, uncovered[:, None, :] * potential, precision=lax.Precision.HIGHEST
    )


def block_sweep(basis, weighted, invert, rhs, near_moments):
    field = jnp.einsum("sklp,skdl->sdp", basis, near_moments, precision=lax.Precision.HIGHEST)
    proj = jnp.einsum("lp,sdp->sdl", weighted, field, precision=lax.Precision.HIGHEST)
    return invert[None, None, :] * (rhs + proj)


def block_charges(ysurf, weights, uncovered, moments):
    surface = jnp.einsum("lp,sdl->sdp", ysurf, moments, precision=lax.Precision.HIGHEST)
    return (surface * (weights[None, None, :] * uncovered[:, None, :])).astype(jnp.bfloat16)


def body(tiles, coefs, centres, radii, neighbours, counts):
    spheres = neighbours.shape[0]
    slots = neighbours.shape[1]
    reach = slots // 2
    aux_local = tiles.shape[0]
    block = tiles.shape[1] // NG
    dirs, weights, ysurf, couple, invert = grid_tables()
    weighted = ysurf * weights[None, :]
    tile_three = tiles.reshape(aux_local, block, NG)
    fit_index = lax.axis_index("fit")
    first_sphere = (lax.axis_index("sph") * lax.axis_size("fit") + fit_index) * spheres
    whole = jnp.einsum("da,acn->cdn", coefs, tile_three, preferred_element_type=jnp.float32)
    whole = lax.psum(whole.reshape(block, NDENS * NG), "fit")
    potential = lax.dynamic_slice_in_dim(whole, fit_index * spheres, spheres, 0)
    potential = potential.reshape(spheres, NDENS, NG)
    geometry = jnp.concatenate([centres, radii[None, :]], axis=0)
    valid = (jnp.arange(slots)[None, :] < counts[:, None]).astype(jnp.float32)
    near_geo = with_halo(geometry, ((("sph", "fit"), 1),), reach)
    local = jnp.clip(neighbours - (first_sphere - reach), 0, spheres + 2 * reach - 1)
    basis, uncovered = block_basis(geometry, near_geo[:, local], valid, dirs, couple)
    rhs = block_rhs(weighted, uncovered, potential)
    moments = invert[None, None, :] * rhs
    for sweep in range(2):
        near_state = with_halo(moments, ((("sph", "fit"), 0),), reach)
        moments = block_sweep(basis, weighted, invert, rhs, near_state[local])
    charges = block_charges(ysurf, weights, uncovered, moments).reshape(spheres, NDENS * NG)
    piece = lax.all_gather(charges, "fit", axis=0, tiled=True)
    rows = piece.shape[0]
    shaped = piece.reshape(rows, NDENS, NG)
    partial_fock = lax.dot_general(
        shaped, tile_three, (((0, 2), (1, 2)), ((), ())), preferred_element_type=jnp.float32
    )
    fock = lax.psum(partial_fock, "sph")
    return (moments, fock)


def solution(mesh):
    placed = (
        P("fit", "sph"),
        P(None, "fit"),
        P(None, ("sph", "fit")),
        P(("sph", "fit")),
        P(("sph", "fit"), None),
        P(("sph", "fit")),
    )
    return jax.shard_map(
        body,
        mesh=mesh,
        in_specs=placed,
        out_specs=(P(("sph", "fit"), None, None), P(None, "fit")),
        check_vma=False,
    )
```

profile of v0, /device:TPU:0, one launch (start us, length us, event | category | flops | bytes accessed | tf_op | source)
XLA Modules:
  0.0 242.6 jit_solution(9293991548820046019)
XLA Ops:
  8.0 4.8 %collective-permute-start = (f32[4,8]{1,0:T(4,128)S(1)}, f32[4,8]{1,0:T(4,128)S(1)}, u32[]{:S(2)}, u32[]{:S(2)}) collective-permute-start(f32[4,8]{1,0:T(4,128)S(1)} %get-tuple-element.90), channel_id=1, source_target_pairs={{0,1},{1,2},{2,3},{3,4},{4,5},{5,6},{6,7},{7,8},{8,9},{9,10},{10,1... | collective-permute-start | bytes 392 | tf_op jit(solution)/shard_map/ppermute | solution.py:22
  12.9 1.4 collective-permute-start.1
  14.3 13.7 %copy.25 = bf16[256,20480]{0,1:T(8,128)(2,1)} copy(bf16[256,20480]{1,0:T(8,128)(2,1)} %param.7) | data formatting | bytes 20971520 | tf_op args[0]
  28.0 7.1 %convolution_bitcast_fusion = f32[64,16,320]{2,1,0:T(8,128)S(1)} fusion(bf16[256,64,320]{0,2,1:T(8,128)(2,1)} %bitcast.208, bf16[16,256]{1,0:T(8,128)(2,1)S(1)} %copy-done), kind=kOutput, calls=%fused_computation.8 | convolution fusion | flops 167772160 | bytes 11804672 | tf_op jit(solution)/shard_map/da,acn->cdn/dot_general | solution.py:140
  35.1 1.6 reshape.3985
  40.2 0.9 multiply_dynamic-update-slice_fusion.47
  41.8 0.8 multiply_dynamic-update-slice_fusion.45
  42.7 0.9 multiply_dynamic-update-slice_fusion.44
  43.6 0.8 multiply_dynamic-update-slice_fusion.43
  44.4 0.9 multiply_dynamic-update-slice_fusion.42
  45.3 0.8 multiply_dynamic-update-slice_fusion.41
  46.2 0.9 multiply_dynamic-update-slice_fusion.40
  47.0 0.9 multiply_dynamic-update-slice_fusion.39
  47.9 0.9 multiply_dynamic-update-slice_fusion.38
  48.8 0.9 multiply_dynamic-update-slice_fusion.37
  49.7 0.9 multiply_dynamic-update-slice_fusion.36
  50.5 0.8 multiply_dynamic-update-slice_fusion.35
  52.2 0.9 multiply_dynamic-update-slice_fusion.33
  53.1 0.9 multiply_dynamic-update-slice_fusion.32
  54.7 0.9 multiply_dynamic-update-slice_fusion.30
  55.7 0.9 multiply_dynamic-update-slice_fusion.29
  56.6 1.0 multiply_dynamic-update-slice_fusion.28
  57.6 1.0 multiply_dynamic-update-slice_fusion.27
  58.5 0.9 multiply_dynamic-update-slice_fusion.26
  59.4 0.8 multiply_dynamic-update-slice_fusion.25
  60.2 0.9 multiply_dynamic-update-slice_fusion.24
  61.1 0.9 multiply_dynamic-update-slice_fusion.23
  62.0 0.8 multiply_dynamic-update-slice_fusion.22
  62.8 0.9 multiply_dynamic-update-slice_fusion.21
  63.7 0.9 multiply_dynamic-update-slice_fusion.20
  64.6 1.0 multiply_dynamic-update-slice_fusion.19
  65.7 1.1 multiply_dynamic-update-slice_fusion.18
  66.7 1.1 multiply_dynamic-update-slice_fusion.17
  67.8 0.9 multiply_dynamic-update-slice_fusion.16
  68.7 0.9 multiply_dynamic-update-slice_fusion.15
  69.6 0.8 multiply_dynamic-update-slice_fusion.14
  70.4 0.9 multiply_dynamic-update-slice_fusion.13
  71.3 0.8 multiply_dynamic-update-slice_fusion.12
  72.9 0.9 multiply_dynamic-update-slice_fusion.10
  73.8 0.9 multiply_dynamic-update-slice_fusion.9
  74.8 1.0 multiply_dynamic-update-slice_fusion.8
  75.8 1.1 multiply_dynamic-update-slice_fusion.7
  76.9 1.1 multiply_dynamic-update-slice_fusion.6
  78.0 1.1 multiply_dynamic-update-slice_fusion.5
  79.4 1.0 multiply_dynamic-update-slice_fusion.4
  80.4 0.9 multiply_dynamic-update-slice_fusion.3
  81.4 0.8 multiply_dynamic-update-slice_fusion.2
  82.2 0.8 multiply_dynamic-update-slice_fusion.1
  83.1 0.9 multiply_dynamic-update-slice_fusion
  83.9 11.8 %all-reduce.2.cloned.1.call-done = f32[64,5120]{1,0:T(8,128)} async-done(((f32[64,5120]{1,0:T(8,128)}), f32[64,5120]{1,0:T(8,128)}) %all-reduce.2.cloned.1.call-update) | async-done | bytes 1310736 | tf_op jit(solution)/shard_map/psum | solution.py:141
  95.7 1.0 constant_dynamic-slice_fusion
  97.4 3.4 %collective-permute-start.2 = (f32[8,16,49]{2,1,0:T(8,128)S(1)}, f32[8,16,49]{2,1,0:T(8,128)S(1)}, u32[]{:S(2)}, u32[]{:S(2)}) collective-permute-start(f32[8,16,49]{2,1,0:T(8,128)S(1)} %get-tuple-element.58), channel_id=1, source_target_pairs={{0,1},{1,2},{2,3},{3,4},{4,5},{5,6},{6,7},{7,8},{8,9},{9,10},{10,1... | collective-permute-start | bytes 75272 | tf_op jit(solution)/shard_map/ppermute | solution.py:22
  100.7 1.5 collective-permute-start.3
  102.2 15.1 %multiply_multiply_fusion = f32[16,16,49,320]{3,1,2,0:T(8,128)} fusion(f32[16,16,49,320]{3,1,2,0:T(8,128)} %multiply_dynamic-update-slice_fusion, f32[16,16,320]{2,1,0:T(8,128)S(1)} %get-tuple-element.55, f32[49]{0:T(128)S(1)} %copy-done.8), kind=kLoop, calls=%fused_computation.7 | loop fusion | flops 8028160 | bytes 32440516 | tf_op jit(solution)/shard_map/mul | solution.py:107
  117.4 1.0 gather_fusion.1
  118.4 28.6 %fusion.4 = f32[16,16,320]{2,1,0:T(8,128)S(1)} fusion(f32[16,16,16,49]{3,2,1,0:T(8,128)S(1)} %bitcast.211, f32[16,16,49,320]{3,1,2,0:T(8,128)} %multiply_multiply_fusion), kind=kOutput, calls=%fused_computation.10 | convolution fusion | flops 770703360 | bytes 17186816 | tf_op jit(solution)/shard_map/sklp,skdl->sdp/dot_general | solution.py:119
  147.5 4.5 %collective-permute-start.4 = (f32[8,16,49]{2,1,0:T(8,128)S(1)}, f32[8,16,49]{2,1,0:T(8,128)S(1)}, u32[]{:S(2)}, u32[]{:S(2)}) collective-permute-start(f32[8,16,49]{2,1,0:T(8,128)S(1)} %get-tuple-element.56), channel_id=1, source_target_pairs={{0,1},{1,2},{2,3},{3,4},{4,5},{5,6},{6,7},{7,8},{8,9},{9,10},{10,1... | collective-permute-start | bytes 75272 | tf_op jit(solution)/shard_map/ppermute | solution.py:22
  152.1 1.5 collective-permute-start.5
  153.9 4.6 %collective-permute-done.5 = f32[8,16,49]{2,1,0:T(8,128)S(1)} collective-permute-done((f32[8,16,49]{2,1,0:T(8,128)S(1)}, f32[8,16,49]{2,1,0:T(8,128)S(1)}, u32[]{:S(2)}, u32[]{:S(2)}) %collective-permute-start.5) | collective-permute-done | bytes 25120 | tf_op jit(solution)/shard_map/ppermute | solution.py:23
  158.5 1.0 gather_fusion.2
  159.6 28.6 %fusion.7 = f32[16,16,320]{2,1,0:T(8,128)S(1)} fusion(f32[16,16,16,49]{3,2,1,0:T(8,128)S(1)} %bitcast.210, f32[16,16,49,320]{3,1,2,0:T(8,128)} %multiply_multiply_fusion), kind=kOutput, calls=%fused_computation.11 | convolution fusion | flops 770703360 | bytes 17186816 | tf_op jit(solution)/shard_map/sklp,skdl->sdp/dot_general | solution.py:119
  189.3 13.8 %all_gather.3 = bf16[64,5120]{1,0:T(8,128)(2,1)S(1)} all-gather(bf16[16,5120]{1,0:T(8,128)(2,1)S(1)} %reshape.3987), channel_id=1, replica_groups=mesh['sph'=8,'fit'=4] {'fit'}, dimensions={0}, use_global_device_ids=true | all-gather | bytes 819200 | tf_op jit(solution)/shard_map/all_gather | solution.py:155
  203.7 5.5 %convolution_bitcast_fusion.1 = f32[16,256]{1,0:T(8,128)S(1)} fusion(bf16[64,16,320]{2,1,0:T(8,128)(2,1)S(1)} %reshape.3988, bf16[256,64,320]{0,2,1:T(8,128)(2,1)} %bitcast.209), kind=kOutput, calls=%fused_computation.20 | convolution fusion | flops 167772160 | bytes 11157504 | tf_op jit(solution)/shard_map/dot_general | solution.py:158
  209.2 26.5 %psum.15 = f32[16,256]{1,0:T(8,128)} all-reduce(f32[16,256]{1,0:T(8,128)S(1)} %convolution_bitcast_fusion.1), channel_id=1, replica_groups=mesh['sph'=8,'fit'=4] {'sph'}, use_global_device_ids=true, to_apply=%region_3.4 | all-reduce | flops 4096 | bytes 32768 | tf_op jit(solution)/shard_map/psum | solution.py:161
  (77 shorter events, 11.0 us)
Async XLA Ops:
  7.2 20.8 %copy-start = (bf16[16,256]{1,0:T(8,128)(2,1)S(1)}, bf16[16,256]{1,0:T(8,128)(2,1)}, u32[]{:S(2)}) copy-start(bf16[16,256]{1,0:T(8,128)(2,1)} %param.8) | copy-start | bytes 24580
  7.2 88.5 %all-reduce.2.cloned.1.call-start = ((), (), s32[]{:S(2)}) async-start(), calls=%async_computation | async-start | bytes 2621440 | tf_op jit(solution)/shard_map/psum | solution.py:141
  8.0 30.6 %collective-permute-start = (f32[4,8]{1,0:T(4,128)S(1)}, f32[4,8]{1,0:T(4,128)S(1)}, u32[]{:S(2)}, u32[]{:S(2)}) collective-permute-start(f32[4,8]{1,0:T(4,128)S(1)} %get-tuple-element.90), channel_id=1, source_target_pairs={{0,1},{1,2},{2,3},{3,4},{4,5},{5,6},{6,7},{7,8},{8,9},{9,10},{10,1... | collective-permute-start | bytes 392 | tf_op jit(solution)/shard_map/ppermute | solution.py:22
  12.8 25.1 %copy-start.5 = (f32[16]{0:T(128)S(1)}, f32[16]{0:T(128)}, u32[]{:S(2)}) copy-start(f32[16]{0:T(128)} %param.10) | copy-start | bytes 196
  12.9 25.2 %copy-start.4 = (s32[16,16]{1,0:T(8,128)S(1)}, s32[16,16]{1,0:T(8,128)}, u32[]{:S(2)}) copy-start(s32[16,16]{1,0:T(8,128)} %param.11) | copy-start | bytes 3076
  12.9 25.3 %copy-start.7 = (s32[16]{0:T(128)S(1)}, s32[16]{0:T(128)}, u32[]{:S(2)}) copy-start(s32[16]{0:T(128)} %param.12) | copy-start | bytes 196
  12.9 25.8 %copy-start.3 = (f32[3,16]{1,0:T(4,128)S(1)}, f32[3,16]{1,0:T(4,128)}, u32[]{:S(2)}) copy-start(f32[3,16]{1,0:T(4,128)} %param.9) | copy-start | bytes 580
  12.9 25.7 %collective-permute-start.1 = (f32[4,8]{1,0:T(4,128)S(1)}, f32[4,8]{1,0:T(4,128)S(1)}, u32[]{:S(2)}, u32[]{:S(2)}) collective-permute-start(f32[4,8]{1,0:T(4,128)S(1)} %get-tuple-element.91), channel_id=1, source_target_pairs={{1,0},{2,1},{3,2},{4,3},{5,4},{6,5},{7,6},{8,7},{9,8},{10,9},{11,1... | collective-permute-start | bytes 392 | tf_op jit(solution)/shard_map/ppermute | solution.py:23
  62.0 34.9 %copy-start.6 = (f32[49]{0:T(128)S(1)}, f32[49]{0:T(128)}, u32[]{:S(2)}) copy-start(f32[49]{0:T(128)} %constant.272) | copy-start | bytes 592
  62.0 40.3 %copy-start.8 = (f32[49]{0:T(128)S(1)}, f32[49]{0:T(128)}, u32[]{:S(2)}) copy-start(f32[49]{0:T(128)} %constant.273) | copy-start | bytes 592
  97.4 20.0 %collective-permute-start.2 = (f32[8,16,49]{2,1,0:T(8,128)S(1)}, f32[8,16,49]{2,1,0:T(8,128)S(1)}, u32[]{:S(2)}, u32[]{:S(2)}) collective-permute-start(f32[8,16,49]{2,1,0:T(8,128)S(1)} %get-tuple-element.58), channel_id=1, source_target_pairs={{0,1},{1,2},{2,3},{3,4},{4,5},{5,6},{6,7},{7,8},{8,9},{9,10},{10,1... | collective-permute-start | bytes 75272 | tf_op jit(solution)/shard_map/ppermute | solution.py:22
  100.7 16.6 %collective-permute-start.3 = (f32[8,16,49]{2,1,0:T(8,128)S(1)}, f32[8,16,49]{2,1,0:T(8,128)S(1)}, u32[]{:S(2)}, u32[]{:S(2)}) collective-permute-start(f32[8,16,49]{2,1,0:T(8,128)S(1)} %get-tuple-element.59), channel_id=1, source_target_pairs={{1,0},{2,1},{3,2},{4,3},{5,4},{6,5},{7,6},{8,7},{9,8},{10,9},{11,1... | collective-permute-start | bytes 75272 | tf_op jit(solution)/shard_map/ppermute | solution.py:23
  147.5 6.4 %collective-permute-start.4 = (f32[8,16,49]{2,1,0:T(8,128)S(1)}, f32[8,16,49]{2,1,0:T(8,128)S(1)}, u32[]{:S(2)}, u32[]{:S(2)}) collective-permute-start(f32[8,16,49]{2,1,0:T(8,128)S(1)} %get-tuple-element.56), channel_id=1, source_target_pairs={{0,1},{1,2},{2,3},{3,4},{4,5},{5,6},{6,7},{7,8},{8,9},{9,10},{10,1... | collective-permute-start | bytes 75272 | tf_op jit(solution)/shard_map/ppermute | solution.py:22
  152.1 6.4 %collective-permute-start.5 = (f32[8,16,49]{2,1,0:T(8,128)S(1)}, f32[8,16,49]{2,1,0:T(8,128)S(1)}, u32[]{:S(2)}, u32[]{:S(2)}) collective-permute-start(f32[8,16,49]{2,1,0:T(8,128)S(1)} %get-tuple-element.57), channel_id=1, source_target_pairs={{1,0},{2,1},{3,2},{4,3},{5,4},{6,5},{7,6},{8,7},{9,8},{10,9},{11,1... | collective-permute-start | bytes 75272 | tf_op jit(solution)/shard_map/ppermute | solution.py:23
  159.5 76.2 %copy-start.1 = (bf16[16,256]{1,0:T(8,128)(2,1)S(1)}, bf16[16,256]{1,0:T(8,128)(2,1)}, u32[]{:S(2)}) copy-start(bf16[16,256]{1,0:T(8,128)(2,1)} %param.8) | copy-start | bytes 24580
  188.6 47.1 %copy-start.2 = (f32[16,16,49]{2,1,0:T(8,128)}, f32[16,16,49]{2,1,0:T(8,128)S(1)}, u32[]{:S(2)}) copy-start(f32[16,16,49]{2,1,0:T(8,128)S(1)} %fusion.11) | copy-start | bytes 150532
Sparse Core Ops, SparseCore 0:
  36.8 58.9 all-reduce.1
where the time goes:
time: 243 us
  matrix products  71.6 us (29%)
  other arithmetic  60.6 us (25%)
  blocking collectives  40.3 us (17%)
  local copies, waits for them, and re-layouts  21.7 us (9%)
  starting transfers between devices  17.2 us (7%)
  waiting for transfers between devices  16.7 us (7%)
  between operations  14.4 us (6%)
    dot_general x2, matrix products, block_sweep(): jnp.einsum('sklp,skdl->sdp', basis, near_moments, precision=lax.Precision...  57.2 us
    unnamed x47, other arithmetic  42.6 us
    psum x1, blocking collectives, body(): fock = lax.psum(partial_fock, 'sph')  26.5 us
    mul x1, other arithmetic, block_basis(): basis = harm * couple[None, None, :, None] * switch[:, :, None, :]  15.1 us
    unnamed x20, local copies, waits for them, and re-layouts  14.5 us
    all_gather x1, blocking collectives, body(): piece = lax.all_gather(charges, 'fit', axis=0, tiled=True)  13.8 us
    ppermute x3, starting transfers between devices, with_halo(): before = lax.ppermute(last, axis, up)  12.8 us
    psum x1, waiting for transfers between devices, body(): whole = lax.psum(whole.reshape(block, NDENS * NG), 'fit')  11.8 us
  transfers between devices with their start and end apart: 7, of which 3 were waited for; matrix products, arithmetic and copies ran while one was open for 35% of the time, Pallas kernels for 0%

commit v1 on v0

--- a/solution.py
+++ b/solution.py
@@ -158,7 +158,8 @@
     partial_fock = lax.dot_general(
         shaped, tile_three, (((0, 2), (1, 2)), ((), ())), preferred_element_type=jnp.float32
     )
-    fock = lax.psum(partial_fock, "sph")
+    parts = lax.all_gather(partial_fock, "sph")
+    fock = jnp.sum(parts, axis=0)
     return (moments, fock)
 
 

time: 243 us -> 232 us (0.955)
  blocking collectives: 40.3 us -> 27.8 us
    psum x1 -> x0, blocking collectives: 26.5 us -> none  [body(): fock = lax.psum(partial_fock, 'sph')]
    all_gather x0 -> x1, blocking collectives: none -> 14 us  [body(): parts = lax.all_gather(partial_fock, 'sph')]
  transfers between devices with their start and end apart: 7 -> 7, of which waited for: 3 -> 3; matrix products, arithmetic and copies ran while one was open for 35% -> 37% of each run, Pallas kernels for 0% -> 0%
where the time goes in v1:
time: 232 us; the launch traced here: 231 us
  matrix products  71.6 us (31%)
  other arithmetic  61.2 us (26%)
  blocking collectives  27.8 us (12%)
  local copies, waits for them, and re-layouts  21.7 us (9%)
  starting transfers between devices  17.2 us (7%)
  waiting for transfers between devices  16.7 us (7%)
  between operations  14.4 us (6%)
    dot_general x2, matrix products, block_sweep(): jnp.einsum('sklp,skdl->sdp', basis, near_moments, precision=lax.Precision...  57.2 us
    unnamed x47, other arithmetic  42.6 us
    mul x1, other arithmetic, block_basis(): basis = harm * couple[None, None, :, None] * switch[:, :, None, :]  15.1 us
    unnamed x20, local copies, waits for them, and re-layouts  14.5 us
    all_gather x1, blocking collectives, body(): parts = lax.all_gather(partial_fock, 'sph')  14 us
    all_gather x1, blocking collectives, body(): piece = lax.all_gather(charges, 'fit', axis=0, tiled=True)  13.8 us
    ppermute x3, starting transfers between devices, with_halo(): before = lax.ppermute(last, axis, up)  12.8 us
    psum x1, waiting for transfers between devices, body(): whole = lax.psum(whole.reshape(block, NDENS * NG), 'fit')  11.8 us
  transfers between devices with their start and end apart: 7, of which 3 were waited for; matrix products, arithmetic and copies ran while one was open for 37% of the time, Pallas kernels for 0%

profile of v1, /device:TPU:0, one launch (start us, length us, event | category | flops | bytes accessed | tf_op | source)
XLA Modules:
  0.0 230.7 jit_solution(10894861587481746320)
XLA Ops:
  8.0 4.8 %collective-permute-start = (f32[4,8]{1,0:T(4,128)S(1)}, f32[4,8]{1,0:T(4,128)S(1)}, u32[]{:S(2)}, u32[]{:S(2)}) collective-permute-start(f32[4,8]{1,0:T(4,128)S(1)} %get-tuple-element.90), channel_id=1, source_target_pairs={{0,1},{1,2},{2,3},{3,4},{4,5},{5,6},{6,7},{7,8},{8,9},{9,10},{10,1... | collective-permute-start | bytes 392 | tf_op jit(solution)/shard_map/ppermute | solution.py:22
  12.9 1.4 collective-permute-start.1
  14.3 13.7 %copy.25 = bf16[256,20480]{0,1:T(8,128)(2,1)} copy(bf16[256,20480]{1,0:T(8,128)(2,1)} %param.7) | data formatting | bytes 20971520 | tf_op args[0]
  28.0 7.1 %convolution_bitcast_fusion = f32[64,16,320]{2,1,0:T(8,128)S(1)} fusion(bf16[256,64,320]{0,2,1:T(8,128)(2,1)} %bitcast.209, bf16[16,256]{1,0:T(8,128)(2,1)S(1)} %copy-done), kind=kOutput, calls=%fused_computation.8 | convolution fusion | flops 167772160 | bytes 11804672 | tf_op jit(solution)/shard_map/da,acn->cdn/dot_general | solution.py:140
  35.1 1.6 reshape.3985
  40.2 0.9 multiply_dynamic-update-slice_fusion.47
  41.8 0.8 multiply_dynamic-update-slice_fusion.45
  42.7 0.9 multiply_dynamic-update-slice_fusion.44
  43.6 0.8 multiply_dynamic-update-slice_fusion.43
  44.4 0.9 multiply_dynamic-update-slice_fusion.42
  45.3 0.8 multiply_dynamic-update-slice_fusion.41
  46.2 0.9 multiply_dynamic-update-slice_fusion.40
  47.0 0.9 multiply_dynamic-update-slice_fusion.39
  47.9 0.9 multiply_dynamic-update-slice_fusion.38
  48.8 0.9 multiply_dynamic-update-slice_fusion.37
  49.7 0.9 multiply_dynamic-update-slice_fusion.36
  50.5 0.8 multiply_dynamic-update-slice_fusion.35
  52.2 0.9 multiply_dynamic-update-slice_fusion.33
  53.1 0.9 multiply_dynamic-update-slice_fusion.32
  54.7 0.9 multiply_dynamic-update-slice_fusion.30
  55.7 0.9 multiply_dynamic-update-slice_fusion.29
  56.6 1.0 multiply_dynamic-update-slice_fusion.28
  57.6 1.0 multiply_dynamic-update-slice_fusion.27
  58.5 0.9 multiply_dynamic-update-slice_fusion.26
  59.4 0.8 multiply_dynamic-update-slice_fusion.25
  60.2 0.9 multiply_dynamic-update-slice_fusion.24
  61.1 0.9 multiply_dynamic-update-slice_fusion.23
  62.0 0.8 multiply_dynamic-update-slice_fusion.22
  62.8 0.9 multiply_dynamic-update-slice_fusion.21
  63.7 0.9 multiply_dynamic-update-slice_fusion.20
  64.6 1.0 multiply_dynamic-update-slice_fusion.19
  65.7 1.1 multiply_dynamic-update-slice_fusion.18
  66.7 1.1 multiply_dynamic-update-slice_fusion.17
  67.8 0.9 multiply_dynamic-update-slice_fusion.16
  68.7 0.9 multiply_dynamic-update-slice_fusion.15
  69.6 0.8 multiply_dynamic-update-slice_fusion.14
  70.4 0.9 multiply_dynamic-update-slice_fusion.13
  71.3 0.8 multiply_dynamic-update-slice_fusion.12
  72.9 0.9 multiply_dynamic-update-slice_fusion.10
  73.8 0.9 multiply_dynamic-update-slice_fusion.9
  74.8 1.0 multiply_dynamic-update-slice_fusion.8
  75.8 1.1 multiply_dynamic-update-slice_fusion.7
  76.9 1.1 multiply_dynamic-update-slice_fusion.6
  78.0 1.1 multiply_dynamic-update-slice_fusion.5
  79.4 1.0 multiply_dynamic-update-slice_fusion.4
  80.4 0.9 multiply_dynamic-update-slice_fusion.3
  81.4 0.8 multiply_dynamic-update-slice_fusion.2
  82.2 0.8 multiply_dynamic-update-slice_fusion.1
  83.1 0.9 multiply_dynamic-update-slice_fusion
  83.9 11.8 %all-reduce.2.cloned.1.call-done = f32[64,5120]{1,0:T(8,128)} async-done(((f32[64,5120]{1,0:T(8,128)}), f32[64,5120]{1,0:T(8,128)}) %all-reduce.2.cloned.1.call-update) | async-done | bytes 1310736 | tf_op jit(solution)/shard_map/psum | solution.py:141
  95.7 1.0 constant_dynamic-slice_fusion
  97.4 3.4 %collective-permute-start.2 = (f32[8,16,49]{2,1,0:T(8,128)S(1)}, f32[8,16,49]{2,1,0:T(8,128)S(1)}, u32[]{:S(2)}, u32[]{:S(2)}) collective-permute-start(f32[8,16,49]{2,1,0:T(8,128)S(1)} %get-tuple-element.58), channel_id=1, source_target_pairs={{0,1},{1,2},{2,3},{3,4},{4,5},{5,6},{6,7},{7,8},{8,9},{9,10},{10,1... | collective-permute-start | bytes 75272 | tf_op jit(solution)/shard_map/ppermute | solution.py:22
  100.7 1.5 collective-permute-start.3
  102.2 15.1 %multiply_multiply_fusion = f32[16,16,49,320]{3,1,2,0:T(8,128)} fusion(f32[16,16,49,320]{3,1,2,0:T(8,128)} %multiply_dynamic-update-slice_fusion, f32[16,16,320]{2,1,0:T(8,128)S(1)} %get-tuple-element.55, f32[49]{0:T(128)S(1)} %copy-done.8), kind=kLoop, calls=%fused_computation.7 | loop fusion | flops 8028160 | bytes 32440516 | tf_op jit(solution)/shard_map/mul | solution.py:107
  117.4 1.0 gather_fusion.1
  118.4 28.6 %fusion.4 = f32[16,16,320]{2,1,0:T(8,128)S(1)} fusion(f32[16,16,16,49]{3,2,1,0:T(8,128)S(1)} %bitcast.212, f32[16,16,49,320]{3,1,2,0:T(8,128)} %multiply_multiply_fusion), kind=kOutput, calls=%fused_computation.10 | convolution fusion | flops 770703360 | bytes 17186816 | tf_op jit(solution)/shard_map/sklp,skdl->sdp/dot_general | solution.py:119
  147.5 4.5 %collective-permute-start.4 = (f32[8,16,49]{2,1,0:T(8,128)S(1)}, f32[8,16,49]{2,1,0:T(8,128)S(1)}, u32[]{:S(2)}, u32[]{:S(2)}) collective-permute-start(f32[8,16,49]{2,1,0:T(8,128)S(1)} %get-tuple-element.56), channel_id=1, source_target_pairs={{0,1},{1,2},{2,3},{3,4},{4,5},{5,6},{6,7},{7,8},{8,9},{9,10},{10,1... | collective-permute-start | bytes 75272 | tf_op jit(solution)/shard_map/ppermute | solution.py:22
  152.1 1.5 collective-permute-start.5
  153.9 4.6 %collective-permute-done.5 = f32[8,16,49]{2,1,0:T(8,128)S(1)} collective-permute-done((f32[8,16,49]{2,1,0:T(8,128)S(1)}, f32[8,16,49]{2,1,0:T(8,128)S(1)}, u32[]{:S(2)}, u32[]{:S(2)}) %collective-permute-start.5) | collective-permute-done | bytes 25120 | tf_op jit(solution)/shard_map/ppermute | solution.py:23
  158.5 1.0 gather_fusion.2
  159.6 28.6 %fusion.7 = f32[16,16,320]{2,1,0:T(8,128)S(1)} fusion(f32[16,16,16,49]{3,2,1,0:T(8,128)S(1)} %bitcast.211, f32[16,16,49,320]{3,1,2,0:T(8,128)} %multiply_multiply_fusion), kind=kOutput, calls=%fused_computation.11 | convolution fusion | flops 770703360 | bytes 17186816 | tf_op jit(solution)/shard_map/sklp,skdl->sdp/dot_general | solution.py:119
  189.3 13.8 %all_gather.9 = bf16[64,5120]{1,0:T(8,128)(2,1)S(1)} all-gather(bf16[16,5120]{1,0:T(8,128)(2,1)S(1)} %reshape.3987), channel_id=1, replica_groups=mesh['sph'=8,'fit'=4] {'fit'}, dimensions={0}, use_global_device_ids=true | all-gather | bytes 819200 | tf_op jit(solution)/shard_map/all_gather | solution.py:155
  203.7 5.5 %convolution_bitcast_fusion.1 = f32[16,256]{1,0:T(8,128)S(1)} fusion(bf16[64,16,320]{2,1,0:T(8,128)(2,1)S(1)} %reshape.3988, bf16[256,64,320]{0,2,1:T(8,128)(2,1)} %bitcast.210), kind=kOutput, calls=%fused_computation.20 | convolution fusion | flops 167772160 | bytes 11157504 | tf_op jit(solution)/shard_map/dot_general | solution.py:158
  209.2 14.0 %all-gather = f32[128,256]{1,0:T(8,128)S(1)} all-gather(f32[16,256]{1,0:T(8,128)S(1)} %convolution_bitcast_fusion.1), channel_id=2, replica_groups=mesh['sph'=8,'fit'=4] {'sph'}, dimensions={0}, use_global_device_ids=true | all-gather | bytes 147456 | tf_op jit(solution)/shard_map/all_gather | solution.py:161
  (78 shorter events, 11.6 us)
Async XLA Ops:
  7.2 20.8 %copy-start = (bf16[16,256]{1,0:T(8,128)(2,1)S(1)}, bf16[16,256]{1,0:T(8,128)(2,1)}, u32[]{:S(2)}) copy-start(bf16[16,256]{1,0:T(8,128)(2,1)} %param.8) | copy-start | bytes 24580
  7.2 88.5 %all-reduce.2.cloned.1.call-start = ((), (), s32[]{:S(2)}) async-start(), calls=%async_computation | async-start | bytes 2621440 | tf_op jit(solution)/shard_map/psum | solution.py:141
  8.0 30.6 %collective-permute-start = (f32[4,8]{1,0:T(4,128)S(1)}, f32[4,8]{1,0:T(4,128)S(1)}, u32[]{:S(2)}, u32[]{:S(2)}) collective-permute-start(f32[4,8]{1,0:T(4,128)S(1)} %get-tuple-element.90), channel_id=1, source_target_pairs={{0,1},{1,2},{2,3},{3,4},{4,5},{5,6},{6,7},{7,8},{8,9},{9,10},{10,1... | collective-permute-start | bytes 392 | tf_op jit(solution)/shard_map/ppermute | solution.py:22
  12.8 25.1 %copy-start.5 = (f32[16]{0:T(128)S(1)}, f32[16]{0:T(128)}, u32[]{:S(2)}) copy-start(f32[16]{0:T(128)} %param.10) | copy-start | bytes 196
  12.9 25.2 %copy-start.4 = (s32[16,16]{1,0:T(8,128)S(1)}, s32[16,16]{1,0:T(8,128)}, u32[]{:S(2)}) copy-start(s32[16,16]{1,0:T(8,128)} %param.11) | copy-start | bytes 3076
  12.9 25.3 %copy-start.7 = (s32[16]{0:T(128)S(1)}, s32[16]{0:T(128)}, u32[]{:S(2)}) copy-start(s32[16]{0:T(128)} %param.12) | copy-start | bytes 196
  12.9 25.8 %copy-start.3 = (f32[3,16]{1,0:T(4,128)S(1)}, f32[3,16]{1,0:T(4,128)}, u32[]{:S(2)}) copy-start(f32[3,16]{1,0:T(4,128)} %param.9) | copy-start | bytes 580
  12.9 25.7 %collective-permute-start.1 = (f32[4,8]{1,0:T(4,128)S(1)}, f32[4,8]{1,0:T(4,128)S(1)}, u32[]{:S(2)}, u32[]{:S(2)}) collective-permute-start(f32[4,8]{1,0:T(4,128)S(1)} %get-tuple-element.91), channel_id=1, source_target_pairs={{1,0},{2,1},{3,2},{4,3},{5,4},{6,5},{7,6},{8,7},{9,8},{10,9},{11,1... | collective-permute-start | bytes 392 | tf_op jit(solution)/shard_map/ppermute | solution.py:23
  62.0 34.9 %copy-start.6 = (f32[49]{0:T(128)S(1)}, f32[49]{0:T(128)}, u32[]{:S(2)}) copy-start(f32[49]{0:T(128)} %constant.272) | copy-start | bytes 592
  62.0 40.3 %copy-start.8 = (f32[49]{0:T(128)S(1)}, f32[49]{0:T(128)}, u32[]{:S(2)}) copy-start(f32[49]{0:T(128)} %constant.273) | copy-start | bytes 592
  97.4 20.0 %collective-permute-start.2 = (f32[8,16,49]{2,1,0:T(8,128)S(1)}, f32[8,16,49]{2,1,0:T(8,128)S(1)}, u32[]{:S(2)}, u32[]{:S(2)}) collective-permute-start(f32[8,16,49]{2,1,0:T(8,128)S(1)} %get-tuple-element.58), channel_id=1, source_target_pairs={{0,1},{1,2},{2,3},{3,4},{4,5},{5,6},{6,7},{7,8},{8,9},{9,10},{10,1... | collective-permute-start | bytes 75272 | tf_op jit(solution)/shard_map/ppermute | solution.py:22
  100.7 16.6 %collective-permute-start.3 = (f32[8,16,49]{2,1,0:T(8,128)S(1)}, f32[8,16,49]{2,1,0:T(8,128)S(1)}, u32[]{:S(2)}, u32[]{:S(2)}) collective-permute-start(f32[8,16,49]{2,1,0:T(8,128)S(1)} %get-tuple-element.59), channel_id=1, source_target_pairs={{1,0},{2,1},{3,2},{4,3},{5,4},{6,5},{7,6},{8,7},{9,8},{10,9},{11,1... | collective-permute-start | bytes 75272 | tf_op jit(solution)/shard_map/ppermute | solution.py:23
  147.5 6.4 %collective-permute-start.4 = (f32[8,16,49]{2,1,0:T(8,128)S(1)}, f32[8,16,49]{2,1,0:T(8,128)S(1)}, u32[]{:S(2)}, u32[]{:S(2)}) collective-permute-start(f32[8,16,49]{2,1,0:T(8,128)S(1)} %get-tuple-element.56), channel_id=1, source_target_pairs={{0,1},{1,2},{2,3},{3,4},{4,5},{5,6},{6,7},{7,8},{8,9},{9,10},{10,1... | collective-permute-start | bytes 75272 | tf_op jit(solution)/shard_map/ppermute | solution.py:22
  152.1 6.4 %collective-permute-start.5 = (f32[8,16,49]{2,1,0:T(8,128)S(1)}, f32[8,16,49]{2,1,0:T(8,128)S(1)}, u32[]{:S(2)}, u32[]{:S(2)}) collective-permute-start(f32[8,16,49]{2,1,0:T(8,128)S(1)} %get-tuple-element.57), channel_id=1, source_target_pairs={{1,0},{2,1},{3,2},{4,3},{5,4},{6,5},{7,6},{8,7},{9,8},{10,9},{11,1... | collective-permute-start | bytes 75272 | tf_op jit(solution)/shard_map/ppermute | solution.py:23
  159.5 64.3 %copy-start.1 = (bf16[16,256]{1,0:T(8,128)(2,1)S(1)}, bf16[16,256]{1,0:T(8,128)(2,1)}, u32[]{:S(2)}) copy-start(bf16[16,256]{1,0:T(8,128)(2,1)} %param.8) | copy-start | bytes 24580
  188.6 35.2 %copy-start.2 = (f32[16,16,49]{2,1,0:T(8,128)}, f32[16,16,49]{2,1,0:T(8,128)S(1)}, u32[]{:S(2)}) copy-start(f32[16,16,49]{2,1,0:T(8,128)S(1)} %fusion.11) | copy-start | bytes 150532
Sparse Core Ops, SparseCore 0:
  36.8 58.9 all-reduce.1
